TPU v7x, 32 devices: a whole 2x2x4 slice. The times are simulated.
32 devices in a mesh: row: 4 (over y, core), col: 8 (over z, x).
Axes of the slice: x: 2, y: 2, z: 4, core: 2. Of those that a mesh axis runs over, the one named last changes fastest.
Arguments:
- inputs: bfloat16 [512, 12288], P('col', 'row'), may hold values from -6 to 6
- grad_out: bfloat16 [512, 12288], P('col', 'row'), may hold values from -6 to 6
- w_in: bfloat16 [12288, 24576], P('row', 'col'), may hold values from -0.0546875 to 0.0546875
- w_out: bfloat16 [24576, 12288], P('col', 'row'), may hold values from -0.0390625 to 0.0390625
Outputs:
- outputs: bfloat16 [512, 12288], P('col', 'row')
- grad_in: bfloat16 [512, 12288], P('col', 'row')
- grad_w_in: bfloat16 [12288, 24576], P('row', 'col')
- grad_w_out: bfloat16 [24576, 12288], P('col', 'row')
All inputs are finite; a program needn't handle non-finite values.
Results may differ from a plain program's by a relative error of at most 0.019.
Values may be sent and summed in bfloat16 or wider, within the bound.
A program may use at most 192 MiB of HBM per device.

v0:
```python
from functools import partial

import jax
import jax.numpy as jnp
from jax import lax
from jax.sharding import PartitionSpec as P


def col_panel(values):
    return lax.all_gather(values, "col", axis=0, tiled=True)


def contract(left, right, dims):
    return lax.dot_general(
        left, right, ((dims[0], dims[1]), ((), ())), preferred_element_type=jnp.float32
    )


def row_sums(left, right, dims):
    return lax.psum_scatter(
        contract(left, right, dims).astype(jnp.bfloat16), "row", scatter_dimension=0, tiled=True
    ).astype(jnp.float32)


def row_spread(values):
    return lax.all_gather(values, "row", axis=0, tiled=True)


def col_sums(left, right, dims):
    return lax.psum_scatter(
        contract(
            lax.dynamic_slice_in_dim(
                left, jnp.int32(0), left.shape[0] // lax.axis_size("col") * lax.axis_size("col"), 0
            ),
            right,
            dims,
        ).astype(jnp.bfloat16),
        "col",
        scatter_dimension=0,
        tiled=True,
    ).astype(jnp.float32)


def local(inputs, grad_out, w_in, w_out):
    gelu_tanh = partial(jax.nn.gelu, approximate=True)
    input_all = col_panel(inputs)
    cotan_all = None
    hidden_pre = row_sums(input_all, w_in, ((1,), (0,)))
    act_all = row_spread(gelu_tanh(hidden_pre).astype(jnp.bfloat16))
    outputs = col_sums(act_all, w_out, ((1,), (0,))).astype(jnp.bfloat16)
    cotan_all = col_panel(grad_out)
    grad_act = row_sums(cotan_all, w_out, ((1,), (1,)))
    grad_pre = jax.vjp(gelu_tanh, hidden_pre)[1](grad_act)[0].astype(jnp.bfloat16)
    grad_pre_all = row_spread(grad_pre)
    grad_w_out = contract(act_all, cotan_all, ((0,), (0,))).astype(jnp.bfloat16)
    grad_w_in = contract(input_all, grad_pre_all, ((0,), (0,))).astype(jnp.bfloat16)
    grad_in = col_sums(grad_pre_all, w_in, ((1,), (1,))).astype(jnp.bfloat16)
    return (outputs, grad_in, grad_w_in, grad_w_out)


def solution(mesh):
    placed = (P("col", "row"), P("col", "row"), P("row", "col"), P("col", "row"))
    return jax.shard_map(
        local,
        mesh=mesh,
        in_specs=placed,
        out_specs=(P("col", "row"), P("col", "row"), P("row", "col"), P("col", "row")),
        check_vma=False,
    )
```

profile of v0, /device:TPU:0, one launch (start us, length us, event | category | flops | bytes accessed | tf_op | source)
XLA Modules:
  0.0 441.4 jit_solution(10468758725500619523)
XLA Ops:
  7.2 0.0 all-gather.9.cloned.1.call-start
  7.2 0.7 all-gather.9.cloned.1.call-update
  7.9 0.0 all-gather.5.cloned.1.call-start
  7.9 0.7 all-gather.5.cloned.1.call-update
  8.6 0.0 reduce-scatter.9.cloned.1.call-start
  8.7 64.7 %all-gather.9.cloned.1.call-done = bf16[512,3072]{1,0:T(8,128)(2,1)} async-done(((bf16[64,3072]{1,0:T(8,128)(2,1)}), bf16[512,3072]{1,0:T(8,128)(2,1)}) %all-gather.9.cloned.1.call-update) | async-done | bytes 3145744 | tf_op jit(solution)/shard_map/all_gather | solution.py:10
  73.4 15.9 %convolution_convert_fusion.2 = bf16[512,3072]{1,0:T(8,128)(2,1)} fusion(bf16[512,3072]{1,0:T(8,128)(2,1)} %all-gather.9.cloned.1.call-done, bf16[3072,3072]{1,0:T(8,128)(2,1)} %param.7), kind=kOutput, calls=%fused_computation.3 | convolution fusion | flops 9665249280 | bytes 25165824 | tf_op jit(solution)/shard_map/dot_general | solution.py:14
  89.2 0.0 reduce-scatter.9.cloned.1.call-update
  89.3 0.0 reduce-scatter.5.cloned.1.call-start
  89.3 45.4 %all-gather.5.cloned.1.call-done = bf16[512,3072]{1,0:T(8,128)(2,1)} async-done(((bf16[64,3072]{1,0:T(8,128)(2,1)}), bf16[512,3072]{1,0:T(8,128)(2,1)}) %all-gather.5.cloned.1.call-update) | async-done | bytes 3145744 | tf_op jit(solution)/shard_map/all_gather | solution.py:10
  134.7 15.8 %convolution_convert_fusion.4 = bf16[512,3072]{1,0:T(8,128)(2,1)} fusion(bf16[512,3072]{1,0:T(8,128)(2,1)} %all-gather.5.cloned.1.call-done, bf16[3072,3072]{1,0:T(8,128)(2,1)} %param.6), kind=kOutput, calls=%fused_computation.5 | convolution fusion | flops 9665249280 | bytes 25165824 | tf_op jit(solution)/shard_map/dot_general | solution.py:14
  150.4 0.0 reduce-scatter.5.cloned.1.call-update
  150.5 0.0 all-gather.7.cloned.1.call-start
  150.5 23.9 %reduce-scatter.9.cloned.1.call-done = bf16[128,3072]{1,0:T(8,128)(2,1)} async-done(((bf16[512,3072]{1,0:T(8,128)(2,1)}), bf16[128,3072]{1,0:T(8,128)(2,1)}) %reduce-scatter.9.cloned.1.call-update) | async-done | bytes 786448 | tf_op jit(solution)/shard_map/reduce_scatter | solution.py:20
  174.4 41.1 %reduce-scatter.5.cloned.1.call-done = bf16[128,3072]{1,0:T(8,128)(2,1)} async-done(((bf16[512,3072]{1,0:T(8,128)(2,1)}), bf16[128,3072]{1,0:T(8,128)(2,1)}) %reduce-scatter.5.cloned.1.call-update) | async-done | bytes 786448 | tf_op jit(solution)/shard_map/reduce_scatter | solution.py:20
  215.5 3.7 fusion.3
  219.2 0.0 all-gather.7.cloned.1.call-update
  219.3 0.0 all-gather.11.cloned.1.call-start
  219.3 0.5 all-gather.11.cloned.1.call-update
  219.8 0.0 reduce-scatter.7.cloned.1.call-start
  219.9 28.1 %all-gather.7.cloned.1.call-done = bf16[512,3072]{1,0:T(8,128)(2,1)} async-done(((bf16[128,3072]{1,0:T(8,128)(2,1)}), bf16[512,3072]{1,0:T(8,128)(2,1)}) %all-gather.7.cloned.1.call-update) | async-done | bytes 3145744 | tf_op jit(solution)/shard_map/all_gather | solution.py:26
  248.0 15.8 %convolution_convert_fusion.3 = bf16[512,3072]{1,0:T(8,128)(2,1)} fusion(bf16[512,3072]{1,0:T(8,128)(2,1)} %all-gather.7.cloned.1.call-done, bf16[3072,3072]{1,0:T(8,128)(2,1)} %param.7), kind=kOutput, calls=%fused_computation.4 | convolution fusion | flops 9665249280 | bytes 25165824 | tf_op jit(solution)/shard_map/dot_general | solution.py:14
  263.8 0.0 reduce-scatter.7.cloned.1.call-update
  263.8 0.2 reduce-scatter.11.cloned.1.call-start
  264.0 14.5 %all-gather.11.cloned.1.call-done = bf16[512,3072]{1,0:T(8,128)(2,1)} async-done(((bf16[128,3072]{1,0:T(8,128)(2,1)}), bf16[512,3072]{1,0:T(8,128)(2,1)}) %all-gather.11.cloned.1.call-update) | async-done | bytes 3145744 | tf_op jit(solution)/shard_map/all_gather | solution.py:26
  278.5 15.9 %convolution_convert_fusion.1 = bf16[512,3072]{1,0:T(8,128)(2,1)} fusion(bf16[512,3072]{1,0:T(8,128)(2,1)} %all-gather.11.cloned.1.call-done, bf16[3072,3072]{1,0:T(8,128)(2,1)} %param.6), kind=kOutput, calls=%fused_computation.2 | convolution fusion | flops 9665249280 | bytes 25165824 | tf_op jit(solution)/shard_map/dot_general | solution.py:14
  294.5 0.0 copy-start.1
  294.5 0.0 reduce-scatter.11.cloned.1.call-update
  294.5 1.9 copy-done.1
  296.4 15.1 %convert_bitcast_fusion = bf16[3072,3072]{0,1:T(8,128)(2,1)} fusion(bf16[512,3072]{1,0:T(8,128)(2,1)} %all-gather.11.cloned.1.call-done, bf16[512,3072]{1,0:T(8,128)(2,1)S(1)} %copy-done.1), kind=kOutput, calls=%fused_computation | convolution fusion | flops 9673113600 | bytes 25165824 | tf_op jit(solution)/shard_map/dot_general | solution.py:14
  311.5 0.0 copy-start
  311.5 24.8 %copy.8 = bf16[3072,3072]{1,0:T(8,128)(2,1)} copy(bf16[3072,3072]{0,1:T(8,128)(2,1)} %convert_bitcast_fusion) | data formatting | bytes 37748736
  336.3 0.0 copy-done
  336.3 15.0 %convolution_convert_fusion = bf16[3072,3072]{1,0:T(8,128)(2,1)} fusion(bf16[512,3072]{1,0:T(8,128)(2,1)} %all-gather.7.cloned.1.call-done, bf16[512,3072]{1,0:T(8,128)(2,1)S(1)} %copy-done), kind=kOutput, calls=%fused_computation.1 | convolution fusion | flops 9673113600 | bytes 25165824 | tf_op jit(solution)/shard_map/dot_general | solution.py:14
  351.3 5.6 %reduce-scatter.7.cloned.1.call-done = bf16[64,3072]{1,0:T(8,128)(2,1)} async-done(((bf16[512,3072]{1,0:T(8,128)(2,1)}), bf16[64,3072]{1,0:T(8,128)(2,1)}) %reduce-scatter.7.cloned.1.call-update) | async-done | bytes 393232 | tf_op jit(solution)/shard_map/reduce_scatter | solution.py:30
  356.9 77.6 %reduce-scatter.11.cloned.1.call-done = bf16[64,3072]{1,0:T(8,128)(2,1)} async-done(((bf16[512,3072]{1,0:T(8,128)(2,1)}), bf16[64,3072]{1,0:T(8,128)(2,1)}) %reduce-scatter.11.cloned.1.call-update) | async-done | bytes 393232 | tf_op jit(solution)/shard_map/reduce_scatter | solution.py:30
Async XLA Ops:
  7.2 66.2 %all-gather.9.cloned.1.call-start = ((), (), s32[]{:S(2)}) async-start(), calls=%async_computation.8 | async-start | bytes 3538944 | tf_op jit(solution)/shard_map/all_gather | solution.py:10
  7.9 126.8 %all-gather.5.cloned.1.call-start = ((), (), s32[]{:S(2)}) async-start(), calls=%async_computation.4 | async-start | bytes 3538944 | tf_op jit(solution)/shard_map/all_gather | solution.py:10
  8.6 165.7 %reduce-scatter.9.cloned.1.call-start = ((), (), s32[]{:S(2)}) async-start(), calls=%async_computation.9 | async-start | bytes 3932160 | tf_op jit(solution)/shard_map/reduce_scatter | solution.py:20
  89.3 126.2 %reduce-scatter.5.cloned.1.call-start = ((), (), s32[]{:S(2)}) async-start(), calls=%async_computation.5 | async-start | bytes 3932160 | tf_op jit(solution)/shard_map/reduce_scatter | solution.py:20
  150.5 97.5 %all-gather.7.cloned.1.call-start = ((), (), s32[]{:S(2)}) async-start(), calls=%async_computation.6 | async-start | bytes 3932160 | tf_op jit(solution)/shard_map/all_gather | solution.py:26
  219.3 59.3 %all-gather.11.cloned.1.call-start = ((), (), s32[]{:S(2)}) async-start(), calls=%async_computation.10 | async-start | bytes 3932160 | tf_op jit(solution)/shard_map/all_gather | solution.py:26
  219.8 137.1 %reduce-scatter.7.cloned.1.call-start = ((), (), s32[]{:S(2)}) async-start(), calls=%async_computation.7 | async-start | bytes 3538944 | tf_op jit(solution)/shard_map/reduce_scatter | solution.py:30
  263.8 170.7 %reduce-scatter.11.cloned.1.call-start = ((), (), s32[]{:S(2)}) async-start(), calls=%async_computation.11 | async-start | bytes 3538944 | tf_op jit(solution)/shard_map/reduce_scatter | solution.py:30
  294.5 1.9 copy-start.1
  311.5 24.8 %copy-start = (bf16[512,3072]{1,0:T(8,128)(2,1)S(1)}, bf16[512,3072]{1,0:T(8,128)(2,1)}, u32[]{:S(2)}) copy-start(bf16[512,3072]{1,0:T(8,128)(2,1)} %all-gather.9.cloned.1.call-done) | copy-start | bytes 9437188
Sparse Core Ops, SparseCore 0:
  10.2 63.1 all-gather.8
  75.5 59.0 all-gather.4
  137.8 36.5 reduce-scatter.8
  177.5 37.9 reduce-scatter.4
  219.4 28.5 all-gather.6
  249.9 28.5 all-gather.10
  282.7 74.2 reduce-scatter.6
  361.1 73.3 reduce-scatter.10
where the time goes:
time: 442 us; the launch traced here: 441 us
  waiting for transfers between devices  303 us (69%)
  matrix products  93.5 us (21%)
  local copies, waits for them, and re-layouts  26.7 us (6%)
  between operations  14.1 us (3%)
    all_gather x2, waiting for transfers between devices, col_panel(): return lax.all_gather(values, 'col', axis=0, tiled=True)  110 us
    dot_general x6, matrix products, contract(): lax.dot_general(left, right, ((dims[0], dims[1]), ((), ())), preferred_el...  93.5 us
    reduce_scatter x2, waiting for transfers between devices, col_sums(): lax.psum_scatter(contract(lax.dynamic_slice_in_dim(left, jnp.int32(0), le...  83.2 us
    reduce_scatter x2, waiting for transfers between devices, row_sums(): lax.psum_scatter(contract(left, right, dims).astype(jnp.bfloat16), 'row',...  65 us
    all_gather x2, waiting for transfers between devices, row_spread(): return lax.all_gather(values, 'row', axis=0, tiled=True)  42.5 us
    unnamed x5, local copies, waits for them, and re-layouts  26.7 us
  transfers between devices with their start and end apart: 8, of which 8 were waited for; matrix products, arithmetic and copies ran while one was open for 27% of the time, Pallas kernels for 0%

commit v1 on v0

v1 whole, which is shorter than its diff:
```python
import functools

import jax
import jax.numpy as jnp
from jax import lax
from jax.experimental import pallas as pl
from jax.experimental.pallas import tpu as pltpu
from jax.sharding import PartitionSpec as P

MESH = pl.DeviceIdType.MESH
NZ = 4
CORES = 2
PARTS = 4
STRIP = 16
VMEM = pl.BlockSpec(memory_space=pltpu.VMEM)
ANY = pl.BlockSpec(memory_space=pl.ANY)


def ring_place(col, nx):
    z, x = col // nx, col % nx
    inner = (x + nx - 1) // nx
    odd = z % 2
    along = (1 - odd) * (x - 1) + odd * (nx - 1 - x)
    return inner * (z * (nx - 1) + along) + (1 - inner) * (NZ * (nx - 1) + NZ - 1 - z)


def ring_col(place, nx):
    back = place // (NZ * (nx - 1))
    z, k = place // (nx - 1), place % (nx - 1)
    odd = z % 2
    x = 1 + (1 - odd) * k + odd * (nx - 2 - k)
    return (1 - back) * (z * nx + x) + back * ((NZ - 1 - (place - NZ * (nx - 1))) * nx)


def greet(axis, others):
    barrier = pltpu.get_barrier_semaphore()
    for other in others:
        pl.semaphore_signal(barrier, inc=1, device_id={axis: other}, device_id_type=MESH)
    pl.semaphore_wait(barrier, len(others))


def rows(start, size):
    return pl.ds(pl.multiple_of(start, STRIP), size)


def col_panels_kernel(n, a_ref, b_ref, a_all, b_all, send_sem, recv_sem, own_sem):
    nx = n // NZ
    place = ring_place(lax.axis_index("col"), nx)
    me = lax.axis_index("col")
    nexts = (ring_col((place + 1) % n, nx), ring_col((place + n - 1) % n, nx))
    size = a_ref.shape[0]
    half = size // 2
    greet("col", nexts)
    streams = [(i, src, dst, d) for i, (src, dst) in enumerate(((a_ref, a_all), (b_ref, b_all))) for d in range(2)]
    own = [pltpu.make_async_copy(src, dst.at[rows(me * size, size)], own_sem.at[i])
           for i, (src, dst) in enumerate(((a_ref, a_all), (b_ref, b_all)))]
    sent = {}
    for step in range(n - 1):
        for i, src, dst, d in streams:
            if step:
                sent[i, d, step - 1].wait_recv()
            origin = ring_col((place + (n - step if d == 0 else step)) % n, nx)
            where = dst.at[rows(origin * size + d * half, half)]
            copy = pltpu.make_async_remote_copy(
                src_ref=where if step else src.at[pl.ds(d * half, half)],
                dst_ref=where,
                send_sem=send_sem.at[i, d, step],
                recv_sem=recv_sem.at[i, d, step],
                device_id={"col": nexts[d]},
                device_id_type=MESH,
            )
            copy.start()
            sent[i, d, step] = copy
        if step == 0:
            for copy in own:
                copy.start()
    for i, _, _, d in streams:
        sent[i, d, n - 2].wait_recv()
    for copy in sent.values():
        copy.wait_send()
    for copy in own:
        copy.wait()


def col_panels(n, a, b):
    full = jax.ShapeDtypeStruct((a.shape[0] * n, a.shape[1]), a.dtype)
    return pl.pallas_call(
        functools.partial(col_panels_kernel, n),
        out_shape=(full, full),
        in_specs=[VMEM, VMEM],
        out_specs=(VMEM, VMEM),
        scratch_shapes=[
            pltpu.SemaphoreType.DMA((2, 2, n - 1)),
            pltpu.SemaphoreType.DMA((2, 2, n - 1)),
            pltpu.SemaphoreType.DMA((2,)),
        ],
        compiler_params=pltpu.CompilerParams(collective_id=0, has_side_effects=True),
    )(a, b)


def hidden_kernel(n, h_ref, g_ref, act_ref, pre_ref, near, far, stage, near_sems, far_sems, y_sems, core_sems):
    ny = n // CORES
    me = lax.axis_index("row")
    y, core = me // CORES, me % CORES
    mate = y * CORES + 1 - core
    up = ((y + 1) % ny) * CORES + core
    down = ((y + ny - 1) % ny) * CORES + core
    greet("row", (mate, up) if ny == 2 else (mate, up, down))
    tokens, wide = h_ref.shape
    size = tokens // n
    width = wide // PARTS
    parts = ((0, h_ref), (1, g_ref))
    columns = [pl.ds(f * width, width) for f in range(PARTS)]

    def send(src, dst, sems, where, device):
        copy = pltpu.make_async_remote_copy(
            src_ref=src, dst_ref=dst, send_sem=sems.at[(0, *where)], recv_sem=sems.at[(1, *where)],
            device_id={"row": device}, device_id_type=MESH)
        copy.start()
        return copy

    copies, near_copies, far_copies = [], {}, {}
    for k in range(ny):
        block = (y + ny - 1 - k) % ny
        for f in range(PARTS):
            for i, ref in parts:
                near_copies[i, k, f] = send(
                    ref.at[rows(((1 - core) * ny + block) * size, size), columns[f]],
                    near.at[i, k, :, columns[f]], near_sems, (i, k, f), mate)

    for k in range(ny - 1):
        base = (core * ny + (y + ny - 1 - k) % ny) * size
        for f in range(PARTS):
            for i, ref in parts:
                near_copies[i, k, f].wait_recv()
                if k:
                    far_copies[i, k - 1, f].wait_recv()

                @pl.loop(0, size // STRIP)
                def _(r):
                    strip = rows(r * STRIP, STRIP)
                    total = ref[rows(base + r * STRIP, STRIP), columns[f]].astype(jnp.float32)
                    total += near[i, k, strip, columns[f]].astype(jnp.float32)
                    if k:
                        total += far[i, k - 1, strip, columns[f]].astype(jnp.float32)
                    stage[i, k, strip, columns[f]] = total.astype(jnp.bfloat16)

                far_copies[i, k, f] = send(
                    stage.at[i, k, :, columns[f]], far.at[i, k, :, columns[f]], far_sems, (i, k, f), up)

    mine = (core * ny + y) * size
    scale = 0.7978845608028654
    ring, swaps = {}, []
    outs = ((0, act_ref), (1, pre_ref))
    for f in range(PARTS):
        for i, _ in parts:
            near_copies[i, ny - 1, f].wait_recv()
            far_copies[i, ny - 2, f].wait_recv()

        @pl.loop(0, size // STRIP)
        def _(r):
            strip = rows(r * STRIP, STRIP)
            full = rows(mine + r * STRIP, STRIP)

            def total(i, ref):
                return (ref[full, columns[f]].astype(jnp.float32)
                        + near[i, ny - 1, strip, columns[f]].astype(jnp.float32)
                        + far[i, ny - 2, strip, columns[f]].astype(jnp.float32))

            v, g = total(0, h_ref), total(1, g_ref)
            square = v * v
            t = jnp.tanh(scale * v * (1.0 + 0.044715 * square))
            act_ref[full, columns[f]] = (0.5 * v * (1.0 + t)).astype(jnp.bfloat16)
            slope = 0.5 * (1.0 + t) + (0.5 * scale) * v * (1.0 - t * t) * (1.0 + 0.134145 * square)
            pre_ref[full, columns[f]] = (slope * g).astype(jnp.bfloat16)

        for i, out in outs:
            where = out.at[rows(mine, size), columns[f]]
            ring[i, 0, f] = send(where, where, y_sems, (i, 0, f), up)
            swaps.append(send(where, where, core_sems, (i, 0, f), mate))
    for k in range(1, ny):
        for f in range(PARTS):
            for i, out in outs:
                ring[i, k - 1, f].wait_recv()
                where = out.at[rows((core * ny + (y + ny - k) % ny) * size, size), columns[f]]
                if k < ny - 1:
                    ring[i, k, f] = send(where, where, y_sems, (i, k, f), up)
                swaps.append(send(where, where, core_sems, (i, k, f), mate))
    for copy in swaps:
        copy.wait()
    for group in (near_copies, far_copies, ring):
        for copy in group.values():
            copy.wait_send()


def hidden(n, h_part, g_part):
    tokens, wide = h_part.shape
    ny, size = n // CORES, tokens // n
    full = jax.ShapeDtypeStruct((tokens, wide), jnp.bfloat16)
    return pl.pallas_call(
        functools.partial(hidden_kernel, n),
        out_shape=(full, full),
        in_specs=[VMEM, VMEM],
        out_specs=(VMEM, VMEM),
        scratch_shapes=[
            pltpu.VMEM((2, ny, size, wide), jnp.bfloat16),
            pltpu.VMEM((2, ny - 1, size, wide), jnp.bfloat16),
            pltpu.VMEM((2, ny - 1, size, wide), jnp.bfloat16),
            pltpu.SemaphoreType.DMA((2, 2, ny, PARTS)),
            pltpu.SemaphoreType.DMA((2, 2, ny - 1, PARTS)),
            pltpu.SemaphoreType.DMA((2, 2, ny - 1, PARTS)),
            pltpu.SemaphoreType.DMA((2, 2, ny, PARTS)),
        ],
        compiler_params=pltpu.CompilerParams(collective_id=1, has_side_effects=True),
    )(h_part, g_part)


def col_sums_kernel(n, a_ref, b_ref, a_out, b_out, held, send_sem, recv_sem):
    nx = n // NZ
    place = ring_place(lax.axis_index("col"), nx)
    me = lax.axis_index("col")
    nexts = (ring_col((place + 1) % n, nx), ring_col((place + n - 1) % n, nx))
    size, wide = a_out.shape
    half = wide // 2
    greet("col", nexts)
    streams = [(i, ref, out, d) for d in range(2) for i, (ref, out) in enumerate(((a_ref, a_out), (b_ref, b_out)))]
    sent = {}
    for step in range(n):
        for i, ref, out, d in streams:
            block = ring_col((place + (2 * n - 1 - step if d == 0 else 1 + step)) % n, nx) if step < n - 1 else me
            columns = pl.ds(d * half, half)
            if step:
                sent[i, d, step - 1].wait_recv()

                @pl.loop(0, size // STRIP)
                def _(r):
                    strip = rows(r * STRIP, STRIP)
                    total = held[i, d, step - 1, strip, :].astype(jnp.float32)
                    total += ref[rows(block * size + r * STRIP, STRIP), columns].astype(jnp.float32)
                    if step < n - 1:
                        held[i, d, step - 1, strip, :] = total.astype(jnp.bfloat16)
                    else:
                        out[strip, columns] = total.astype(jnp.bfloat16)

            if step < n - 1:
                copy = pltpu.make_async_remote_copy(
                    src_ref=held.at[i, d, step - 1] if step else ref.at[rows(block * size, size), columns],
                    dst_ref=held.at[i, d, step],
                    send_sem=send_sem.at[i, d, step],
                    recv_sem=recv_sem.at[i, d, step],
                    device_id={"col": nexts[d]},
                    device_id_type=MESH,
                )
                copy.start()
                sent[i, d, step] = copy
    for copy in sent.values():
        copy.wait_send()


def col_sums(n, a, b):
    size, wide = a.shape[0] // n, a.shape[1]
    part = jax.ShapeDtypeStruct((size, wide), jnp.bfloat16)
    return pl.pallas_call(
        functools.partial(col_sums_kernel, n),
        out_shape=(part, part),
        in_specs=[VMEM, VMEM],
        out_specs=(VMEM, VMEM),
        scratch_shapes=[
            pltpu.VMEM((2, 2, n - 1, size, wide // 2), jnp.bfloat16),
            pltpu.SemaphoreType.DMA((2, 2, n - 1)),
            pltpu.SemaphoreType.DMA((2, 2, n - 1)),
        ],
        compiler_params=pltpu.CompilerParams(collective_id=2, has_side_effects=True),
    )(a, b)


def contract(left, right, dims):
    return lax.dot_general(
        left, right, ((dims[0], dims[1]), ((), ())), preferred_element_type=jnp.float32
    ).astype(jnp.bfloat16)


def solution(mesh):
    n_row, n_col = mesh.shape["row"], mesh.shape["col"]

    def local(inputs, grad_out, w_in, w_out):
        input_all, cotan_all = col_panels(n_col, inputs, grad_out)
        act_all, grad_pre_all = hidden(
            n_row,
            contract(input_all, w_in, ((1,), (0,))),
            contract(cotan_all, w_out, ((1,), (1,))),
        )
        outputs, grad_in = col_sums(
            n_col,
            contract(act_all, w_out, ((1,), (0,))),
            contract(grad_pre_all, w_in, ((1,), (1,))),
        )
        grad_w_out = contract(act_all, cotan_all, ((0,), (0,)))
        grad_w_in = contract(input_all, grad_pre_all, ((0,), (0,)))
        return (outputs, grad_in, grad_w_in, grad_w_out)

    placed = (P("col", "row"), P("col", "row"), P("row", "col"), P("col", "row"))
    return jax.shard_map(local, mesh=mesh, in_specs=placed, out_specs=placed, check_vma=False)
```

time: 442 us -> 310 us (0.70)
  waiting for transfers between devices: 303 us -> 0 us
  Pallas kernels: 0 us -> 216 us
  local copies, waits for them, and re-layouts: 26.7 us -> 1.51 us
  between operations: 14.1 us -> 0.69 us
    pallas_call x0 -> x3, Pallas kernels: none -> 216 us  [the longest x1 79.3 us: hidden(): pl.pallas_call(functools.partial(hidden_kernel, n), out_shape=(full, full...]
    all_gather x4 -> x0, waiting for transfers between devices: 153 us -> none  [the longest x2 110 us: col_panel(): return lax.all_gather(values, 'col', axis=0, tiled=True)]
    reduce_scatter x4 -> x0, waiting for transfers between devices: 148 us -> none  [the longest x2 83.2 us: col_sums(): lax.psum_scatter(contract(lax.dynamic_slice_in_dim(left, jnp.int32(0), le...]
    unnamed x5 -> x12, local copies, waits for them, and re-layouts: 26.7 us -> 1.51 us
  transfers between devices with their start and end apart: 8 -> 0, of which waited for: 8 -> 0; matrix products, arithmetic and copies ran while one was open for 27% -> 0% of each run, Pallas kernels for 0% -> 0%
where the time goes in v1:
time: 310 us
  Pallas kernels  216 us (70%)
  matrix products  91.9 us (30%)
    dot_general x6, matrix products, contract(): lax.dot_general(left, right, ((dims[0], dims[1]), ((), ())), preferred_el...  91.9 us
    pallas_call x1, Pallas kernels, hidden(): pl.pallas_call(functools.partial(hidden_kernel, n), out_shape=(full, full...  79.3 us
    pallas_call x1, Pallas kernels, col_sums(): pl.pallas_call(functools.partial(col_sums_kernel, n), out_shape=(part, pa...  68.4 us
    pallas_call x1, Pallas kernels, col_panels(): pl.pallas_call(functools.partial(col_panels_kernel, n), out_shape=(full,...  68.3 us

profile of v1, /device:TPU:0, one launch (start us, length us, event | category | flops | bytes accessed | tf_op | source)
XLA Modules:
  0.0 310.1 jit_solution(16111119754306420441)
XLA Ops:
  0.6 68.3 %shard_map.75 = (bf16[512,3072]{1,0:T(8,128)(2,1)}, bf16[512,3072]{1,0:T(8,128)(2,1)}) custom-call(bf16[64,3072]{1,0:T(8,128)(2,1)} %a_ref.1, bf16[64,3072]{1,0:T(8,128)(2,1)} %b_ref.1), custom_call_target="tpu_custom_call" | custom-call | tf_op jit(solution)/shard_map/pallas_call | solution.py:87
  69.0 0.0 copy-start.2
  69.0 16.0 %convolution_convert_fusion.5.h_ref = bf16[512,3072]{1,0:T(8,128)(2,1)} fusion(bf16[512,3072]{1,0:T(8,128)(2,1)} %get-tuple-element.10, bf16[3072,3072]{1,0:T(8,128)(2,1)} %param.6), kind=kOutput, calls=%fused_computation.5 | convolution fusion | flops 9665249280 | bytes 25165824 | tf_op jit(solution)/shard_map/dot_general | solution.py:278
  84.9 0.0 copy-done.2
  84.9 15.0 %convolution_convert_fusion.4.g_ref = bf16[512,3072]{1,0:T(8,128)(2,1)} fusion(bf16[512,3072]{1,0:T(8,128)(2,1)S(1)} %copy-done.2, bf16[3072,3072]{1,0:T(8,128)(2,1)} %param.7), kind=kOutput, calls=%fused_computation.4 | convolution fusion | flops 9665249280 | bytes 25165824 | tf_op jit(solution)/shard_map/dot_general | solution.py:278
  99.9 79.3 %shard_map.76 = (bf16[512,3072]{1,0:T(8,128)(2,1)}, bf16[512,3072]{1,0:T(8,128)(2,1)}) custom-call(bf16[512,3072]{1,0:T(8,128)(2,1)} %convolution_convert_fusion.5.h_ref, bf16[512,3072]{1,0:T(8,128)(2,1)} %convolution_convert_fusion.4.g_ref), custom_call_target="tpu_custom_call" | custom-call | tf_op jit(solution)/shard_map/pallas_call | solution.py:200
  179.2 0.0 copy-start.4
  179.2 16.0 %convolution_convert_fusion.3.a_ref = bf16[512,3072]{1,0:T(8,128)(2,1)} fusion(bf16[512,3072]{1,0:T(8,128)(2,1)} %get-tuple-element.12, bf16[3072,3072]{1,0:T(8,128)(2,1)} %param.7), kind=kOutput, calls=%fused_computation.3 | convolution fusion | flops 9665249280 | bytes 25165824 | tf_op jit(solution)/shard_map/dot_general | solution.py:278
  195.2 0.0 copy-done.4
  195.2 15.0 %convolution_convert_fusion.2.b_ref = bf16[512,3072]{1,0:T(8,128)(2,1)} fusion(bf16[512,3072]{1,0:T(8,128)(2,1)S(1)} %copy-done.4, bf16[3072,3072]{1,0:T(8,128)(2,1)} %param.6), kind=kOutput, calls=%fused_computation.2 | convolution fusion | flops 9665249280 | bytes 25165824 | tf_op jit(solution)/shard_map/dot_general | solution.py:278
  210.2 68.4 %shard_map.77 = (bf16[64,3072]{1,0:T(8,128)(2,1)}, bf16[64,3072]{1,0:T(8,128)(2,1)}) custom-call(bf16[512,3072]{1,0:T(8,128)(2,1)} %convolution_convert_fusion.3.a_ref, bf16[512,3072]{1,0:T(8,128)(2,1)} %convolution_convert_fusion.2.b_ref), custom_call_target="tpu_custom_call" | custom-call | tf_op jit(solution)/shard_map/pallas_call | solution.py:263
  278.6 0.0 copy-start.3
  278.6 16.5 %convolution_convert_fusion.1 = bf16[3072,3072]{1,0:T(8,128)(2,1)} fusion(bf16[512,3072]{1,0:T(8,128)(2,1)} %get-tuple-element.10, bf16[512,3072]{1,0:T(8,128)(2,1)} %get-tuple-element.13), kind=kOutput, calls=%fused_computation.1 | convolution fusion | flops 9673113600 | bytes 25165824 | tf_op jit(solution)/shard_map/dot_general | solution.py:278
  295.1 0.0 copy-done.3
  295.1 0.0 copy-start.1
  295.1 0.0 copy-start
  295.1 13.5 %convolution_convert_fusion = bf16[3072,3072]{1,0:T(8,128)(2,1)} fusion(bf16[512,3072]{1,0:T(8,128)(2,1)S(1)} %copy-done.3, bf16[512,3072]{1,0:T(8,128)(2,1)S(1)} %copy-done.2), kind=kOutput, calls=%fused_computation | convolution fusion | flops 9673113600 | bytes 25165824 | tf_op jit(solution)/shard_map/dot_general | solution.py:278
  308.6 0.0 copy-done.1
  308.6 0.7 copy.10
  309.4 0.0 copy-done
  309.4 0.7 copy.11
Async XLA Ops:
  69.0 16.0 %copy-start.2 = (bf16[512,3072]{1,0:T(8,128)(2,1)S(1)}, bf16[512,3072]{1,0:T(8,128)(2,1)}, u32[]{:S(2)}) copy-start(bf16[512,3072]{1,0:T(8,128)(2,1)} %get-tuple-element.11) | copy-start | bytes 9437188
  179.2 16.0 %copy-start.4 = (bf16[512,3072]{1,0:T(8,128)(2,1)S(1)}, bf16[512,3072]{1,0:T(8,128)(2,1)}, u32[]{:S(2)}) copy-start(bf16[512,3072]{1,0:T(8,128)(2,1)} %get-tuple-element.13) | copy-start | bytes 9437188
  278.6 16.5 %copy-start.3 = (bf16[512,3072]{1,0:T(8,128)(2,1)S(1)}, bf16[512,3072]{1,0:T(8,128)(2,1)}, u32[]{:S(2)}) copy-start(bf16[512,3072]{1,0:T(8,128)(2,1)} %get-tuple-element.12) | copy-start | bytes 9437188
  295.1 13.5 %copy-start.1 = (bf16[64,3072]{1,0:T(8,128)(2,1)S(1)}, bf16[64,3072]{1,0:T(8,128)(2,1)}, u32[]{:S(2)}) copy-start(bf16[64,3072]{1,0:T(8,128)(2,1)} %get-tuple-element.20) | copy-start | bytes 1179652
  295.1 14.3 %copy-start = (bf16[64,3072]{1,0:T(8,128)(2,1)S(1)}, bf16[64,3072]{1,0:T(8,128)(2,1)}, u32[]{:S(2)}) copy-start(bf16[64,3072]{1,0:T(8,128)(2,1)} %get-tuple-element.21) | copy-start | bytes 1179652

commit v2 on v0

v2 whole, which is shorter than its diff:
```python
import functools

import jax
import jax.numpy as jnp
from jax import lax
from jax.experimental import pallas as pl
from jax.experimental.pallas import tpu as pltpu
from jax.sharding import PartitionSpec as P

MESH = pl.DeviceIdType.MESH
NZ = 4
CORES = 2
PARTS = 4
SUBS = 2
LANES = 256
STRIP = 16
VMEM = pl.BlockSpec(memory_space=pltpu.VMEM)
ANY = pl.BlockSpec(memory_space=pl.ANY)


def ring_place(col, nx):
    z, x = col // nx, col % nx
    inner = (x + nx - 1) // nx
    odd = z % 2
    along = (1 - odd) * (x - 1) + odd * (nx - 1 - x)
    return inner * (z * (nx - 1) + along) + (1 - inner) * (NZ * (nx - 1) + NZ - 1 - z)


def ring_col(place, nx):
    back = place // (NZ * (nx - 1))
    z, k = place // (nx - 1), place % (nx - 1)
    odd = z % 2
    x = 1 + (1 - odd) * k + odd * (nx - 2 - k)
    return (1 - back) * (z * nx + x) + back * ((NZ - 1 - (place - NZ * (nx - 1))) * nx)


def greet(others):
    barrier = pltpu.get_barrier_semaphore()
    for other in others:
        pl.semaphore_signal(barrier, inc=1, device_id=other, device_id_type=MESH)
    pl.semaphore_wait(barrier, len(others))


def rows(start, size):
    return pl.ds(pl.multiple_of(start, STRIP), size)


def layer_kernel(
    n_row, n_col, x_ref, c_ref, w_in, w_out, x_all, c_all, act_ref, pre_ref, out_ref, gin_ref,
    h_ref, g_ref, o_ref, i_ref, near, far, stage, slope_ref, held, by_col, by_row,
    own_sem, w_sem, ag_sems, near_sems, far_sems, y_sems, core_sems, rs_sems,
):
    nx, ny = n_col // NZ, n_row // CORES
    here = lax.axis_index("col")
    place = ring_place(here, nx)
    nexts = [{"col": ring_col((place + 1) % n_col, nx)}, {"col": ring_col((place + n_col - 1) % n_col, nx)}]
    me = lax.axis_index("row")
    y, core = me // CORES, me % CORES
    mate = {"row": y * CORES + 1 - core}
    up = {"row": ((y + 1) % ny) * CORES + core}
    down = {"row": ((y + ny - 1) % ny) * CORES + core}
    greet(nexts + [mate, up] + ([] if ny == 2 else [down]))
    size, wide = x_ref.shape
    tokens = x_all.shape[0]
    fine = tokens // n_row
    width = wide // PARTS
    lanes = LANES if width % LANES == 0 else LANES // 2
    columns = [pl.ds(f * width, width) for f in range(PARTS)]
    loose = []

    def send(src, dst, sems, where, device):
        copy = pltpu.make_async_remote_copy(
            src_ref=src, dst_ref=dst, send_sem=sems.at[(0, *where)], recv_sem=sems.at[(1, *where)],
            device_id=device, device_id_type=MESH)
        copy.start()
        loose.append(copy)
        return copy

    def gather(i, src, dst):
        piece = size // (2 * SUBS)
        flows = [(d, s) for s in range(SUBS) for d in range(2)]
        last = {}
        for step in range(n_col - 1):
            for d, s in flows:
                if step:
                    last[d, s].wait_recv()
                at = (d * SUBS + s) * piece
                origin = ring_col((place + (n_col - step if d == 0 else step)) % n_col, nx)
                where = dst.at[rows(origin * size + at, piece)]
                last[d, s] = send(where if step else src.at[pl.ds(at, piece)], where, ag_sems, (i, d, s, step), nexts[d])
            if step == 0:
                own = pltpu.make_async_copy(src, dst.at[rows(here * size, size)], own_sem.at[i])
                own.start()
            yield
        for copy in last.values():
            copy.wait_recv()
        own.wait()
        yield

    tiles = []
    for kind, weight in ((0, w_in), (1, w_out), (0, w_out), (1, w_in)):
        for f in range(PARTS):
            tiles.append((kind, f % 2, weight.at[:, columns[f]] if kind == 0 else weight.at[columns[f], :]))

    def fetch(j):
        kind, slot, src = tiles[j]
        return pltpu.make_async_copy(src, (by_row if kind else by_col).at[slot], w_sem.at[kind, slot])

    def product(j, left, dst):
        kind, slot, _ = tiles[j]
        fetch(j).wait()
        if j + 1 < len(tiles):
            fetch(j + 1).start()
        f = j % PARTS

        @pl.loop(0, width // lanes)
        def _(t):
            at = pl.ds(pl.multiple_of(t * lanes, lanes), lanes)
            right = by_row[slot, at, :] if kind else by_col[slot, :, at]
            total = lax.dot_general(left[...], right, (((1,), (kind,)), ((), ())),
                                    preferred_element_type=jnp.float32)
            dst[:, pl.ds(pl.multiple_of(f * width + t * lanes, lanes), lanes)] = total.astype(jnp.bfloat16)

    scale = 0.7978845608028654
    swaps = {0: [], 1: []}

    def exchange(i, f, ref, out):
        cols = columns[f]
        got_near, got_far, ring = [], [], []
        for k in range(ny):
            block = (y + ny - 1 - k) % ny
            got_near.append(send(ref.at[rows(((1 - core) * ny + block) * fine, fine), cols],
                                 near.at[i, k, :, cols], near_sems, (i, k, f), mate))
        yield
        for k in range(ny - 1):
            base = (core * ny + (y + ny - 1 - k) % ny) * fine
            got_near[k].wait_recv()
            if k:
                got_far[k - 1].wait_recv()

            @pl.loop(0, fine // STRIP)
            def _(r):
                strip = rows(r * STRIP, STRIP)
                total = ref[rows(base + r * STRIP, STRIP), cols].astype(jnp.float32)
                total += near[i, k, strip, cols].astype(jnp.float32)
                if k:
                    total += far[i, k - 1, strip, cols].astype(jnp.float32)
                stage[i, k, strip, cols] = total.astype(jnp.bfloat16)

            got_far.append(send(stage.at[i, k, :, cols], far.at[i, k, :, cols], far_sems, (i, k, f), up))
            yield
        got_near[ny - 1].wait_recv()
        got_far[ny - 2].wait_recv()
        mine = (core * ny + y) * fine

        @pl.loop(0, fine // STRIP)
        def _(r):
            strip = rows(r * STRIP, STRIP)
            full = rows(mine + r * STRIP, STRIP)
            v = (ref[full, cols].astype(jnp.float32) + near[i, ny - 1, strip, cols].astype(jnp.float32)
                 + far[i, ny - 2, strip, cols].astype(jnp.float32))
            if i == 0:
                square = v * v
                t = jnp.tanh(scale * v * (1.0 + 0.044715 * square))
                out[full, cols] = (0.5 * v * (1.0 + t)).astype(jnp.bfloat16)
                slope_ref[strip, cols] = (
                    0.5 * (1.0 + t) + (0.5 * scale) * v * (1.0 - t * t) * (1.0 + 0.134145 * square))
            else:
                out[full, cols] = (slope_ref[strip, cols] * v).astype(jnp.bfloat16)

        where = out.at[rows(mine, fine), cols]
        ring.append(send(where, where, y_sems, (i, 0, f), up))
        swaps[i].append(send(where, where, core_sems, (i, 0, f), mate))
        yield
        for k in range(1, ny):
            ring[k - 1].wait_recv()
            where = out.at[rows((core * ny + (y + ny - k) % ny) * fine, fine), cols]
            if k < ny - 1:
                ring.append(send(where, where, y_sems, (i, k, f), up))
            swaps[i].append(send(where, where, core_sems, (i, k, f), mate))
            yield

    def reduce(i, f, ref, out):
        d, cols = f % 2, columns[f]
        copy = None
        for step in range(n_col):
            final = step == n_col - 1
            block = here if final else ring_col((place + (2 * n_col - 1 - step if d == 0 else 1 + step)) % n_col, nx)
            if step:
                copy.wait_recv()

                @pl.loop(0, size // STRIP)
                def _(r):
                    strip = rows(r * STRIP, STRIP)
                    total = held[i, f, step - 1, strip, :].astype(jnp.float32)
                    total += ref[rows(block * size + r * STRIP, STRIP), cols].astype(jnp.float32)
                    if final:
                        out[strip, cols] = total.astype(jnp.bfloat16)
                    else:
                        held[i, f, step - 1, strip, :] = total.astype(jnp.bfloat16)

            if not final:
                copy = send(held.at[i, f, step - 1] if step else ref.at[rows(block * size, size), cols],
                            held.at[i, f, step], rs_sems, (i, f, step), nexts[d])
            yield

    def go(*flows):
        for flow in flows:
            next(flow, None)

    def drain(flows):
        for _ in range(n_col + 2):
            go(*flows)

    fetch(0).start()
    inward = gather(0, x_ref, x_all)
    for _ in range(n_col):
        go(inward)
    other = gather(1, c_ref, c_all)
    acts = [exchange(0, f, h_ref, act_ref) for f in range(PARTS)]
    pres = [exchange(1, f, g_ref, pre_ref) for f in range(PARTS)]
    outs = [reduce(0, f, o_ref, out_ref) for f in range(PARTS)]
    gins = [reduce(1, f, i_ref, gin_ref) for f in range(PARTS)]
    go(other)
    for f in range(PARTS):
        product(f, x_all, h_ref)
        go(acts[f], *acts[f - 1:f], other)
    go(acts[-1])
    for _ in range(ny - 2):
        go(*acts)
    for f in range(PARTS):
        go(acts[f], other)
    for _ in range(n_col):
        go(other)
    for f in range(PARTS):
        product(PARTS + f, c_all, g_ref)
        go(pres[f], *pres[f - 1:f], acts[f])
    go(pres[-1])
    for _ in range(ny - 2):
        go(*acts)
        go(*pres)
    for copy in swaps[0]:
        copy.wait_recv()
    for f in range(PARTS):
        product(2 * PARTS + f, act_ref, o_ref)
        go(outs[f], pres[f], *outs[:f])
    for _ in range(ny - 1):
        for f in range(PARTS):
            go(pres[f], outs[f])
    for copy in swaps[1]:
        copy.wait_recv()
    for f in range(PARTS):
        product(3 * PARTS + f, pre_ref, i_ref)
        go(gins[f], *outs, *gins[:f])
    drain(outs + gins)
    for copy in loose:
        copy.wait_send()


def layer(n_row, n_col, x, c, w_in, w_out):
    size, wide = x.shape
    tokens = size * n_col
    ny, fine = n_row // CORES, tokens // n_row
    width = wide // PARTS
    full = jax.ShapeDtypeStruct((tokens, wide), jnp.bfloat16)
    part = jax.ShapeDtypeStruct((size, wide), jnp.bfloat16)
    dma = pltpu.SemaphoreType.DMA
    half = functools.partial(pltpu.VMEM, dtype=jnp.bfloat16)
    return pl.pallas_call(
        functools.partial(layer_kernel, n_row, n_col),
        out_shape=(full, full, full, full, part, part),
        in_specs=[VMEM, VMEM, ANY, ANY],
        out_specs=(VMEM,) * 6,
        scratch_shapes=[
            half((tokens, wide)), half((tokens, wide)), half((tokens, wide)), half((tokens, wide)),
            half((2, ny, fine, wide)),
            half((2, ny - 1, fine, wide)),
            half((2, ny - 1, fine, wide)),
            pltpu.VMEM((fine, wide), jnp.float32),
            half((2, PARTS, n_col - 1, size, width)),
            half((2, wide, width)),
            half((2, width, wide)),
            dma((2,)),
            dma((2, 2)),
            dma((2, 2, 2, SUBS, n_col - 1)),
            dma((2, 2, ny, PARTS)),
            dma((2, 2, ny - 1, PARTS)),
            dma((2, 2, ny - 1, PARTS)),
            dma((2, 2, ny, PARTS)),
            dma((2, 2, PARTS, n_col - 1)),
        ],
        compiler_params=pltpu.CompilerParams(
            collective_id=0, has_side_effects=True, vmem_limit_bytes=67043328),
    )(x, c, w_in, w_out)


def contract(left, right, dims):
    return lax.dot_general(
        left, right, ((dims[0], dims[1]), ((), ())), preferred_element_type=jnp.float32
    ).astype(jnp.bfloat16)


def solution(mesh):
    n_row, n_col = mesh.shape["row"], mesh.shape["col"]

    def local(inputs, grad_out, w_in, w_out):
        input_all, cotan_all, act_all, grad_pre_all, outputs, grad_in = layer(
            n_row, n_col, inputs, grad_out, w_in, w_out)
        grad_w_out = contract(act_all, cotan_all, ((0,), (0,)))
        grad_w_in = contract(input_all, grad_pre_all, ((0,), (0,)))
        return (outputs, grad_in, grad_w_in, grad_w_out)

    placed = (P("col", "row"), P("col", "row"), P("row", "col"), P("col", "row"))
    return jax.shard_map(local, mesh=mesh, in_specs=placed, out_specs=placed, check_vma=False)
```

time: 442 us -> 216 us (0.49)
  waiting for transfers between devices: 303 us -> 0 us
  Pallas kernels: 0 us -> 184 us
  matrix products: 93.5 us -> 29.8 us
  local copies, waits for them, and re-layouts: 26.7 us -> 1.51 us
  between operations: 14.1 us -> 0.67 us
    pallas_call x0 -> x1, Pallas kernels: none -> 184 us  [layer(): pl.pallas_call(functools.partial(layer_kernel, n_row, n_col), out_shape=(...]
    all_gather x4 -> x0, waiting for transfers between devices: 153 us -> none  [the longest x2 110 us: col_panel(): return lax.all_gather(values, 'col', axis=0, tiled=True)]
    reduce_scatter x4 -> x0, waiting for transfers between devices: 148 us -> none  [the longest x2 83.2 us: col_sums(): lax.psum_scatter(contract(lax.dynamic_slice_in_dim(left, jnp.int32(0), le...]
    dot_general x6 -> x2, matrix products: 93.5 us -> 29.8 us  [contract(): lax.dot_general(left, right, ((dims[0], dims[1]), ((), ())), preferred_el...]
    unnamed x5 -> x10, local copies, waits for them, and re-layouts: 26.7 us -> 1.51 us
  transfers between devices with their start and end apart: 8 -> 0, of which waited for: 8 -> 0; matrix products, arithmetic and copies ran while one was open for 27% -> 0% of each run, Pallas kernels for 0% -> 0%
where the time goes in v2:
time: 216 us
  Pallas kernels  184 us (85%)
  matrix products  29.8 us (14%)
    pallas_call x1, Pallas kernels, layer(): pl.pallas_call(functools.partial(layer_kernel, n_row, n_col), out_shape=(...  184 us
    dot_general x2, matrix products, contract(): lax.dot_general(left, right, ((dims[0], dims[1]), ((), ())), preferred_el...  29.8 us

profile of v2, /device:TPU:0, one launch (start us, length us, event | category | flops | bytes accessed | tf_op | source)
XLA Modules:
  0.0 215.6 jit_solution(4837819312894106606)
XLA Ops:
  0.6 183.6 %shard_map.75 = (bf16[512,3072]{1,0:T(8,128)(2,1)}, bf16[512,3072]{1,0:T(8,128)(2,1)}, bf16[512,3072]{1,0:T(8,128)(2,1)}, bf16[512,3072]{1,0:T(8,128)(2,1)}, bf1...) custom-call(bf16[64,3072]{1,0:T(8,128)(2,1)} %x_ref.1, bf16[64,3072]{1,0:T(8,128)(2,1)} %c_ref.1, ...), custom_call_target="tpu_custom_call" | custom-call | tf_op jit(solution)/shard_map/pallas_call | solution.py:269
  184.2 0.0 copy-start.2
  184.2 0.0 copy-start.3
  184.2 16.5 %convolution_convert_fusion.1 = bf16[3072,3072]{1,0:T(8,128)(2,1)} fusion(bf16[512,3072]{1,0:T(8,128)(2,1)} %get-tuple-element.12, bf16[512,3072]{1,0:T(8,128)(2,1)} %get-tuple-element.13), kind=kOutput, calls=%fused_computation.1 | convolution fusion | flops 9673113600 | bytes 25165824 | tf_op jit(solution)/shard_map/dot_general | solution.py:298
  200.7 0.0 copy-done.2
  200.7 0.0 copy-done.3
  200.7 0.0 copy-start.1
  200.7 0.0 copy-start
  200.7 13.3 %convolution_convert_fusion = bf16[3072,3072]{1,0:T(8,128)(2,1)} fusion(bf16[512,3072]{1,0:T(8,128)(2,1)S(1)} %copy-done.3, bf16[512,3072]{1,0:T(8,128)(2,1)S(1)} %copy-done.2), kind=kOutput, calls=%fused_computation | convolution fusion | flops 9673113600 | bytes 25165824 | tf_op jit(solution)/shard_map/dot_general | solution.py:298
  214.1 0.0 copy-done.1
  214.1 0.7 copy.10
  214.8 0.0 copy-done
  214.8 0.7 copy.11
Async XLA Ops:
  184.2 16.5 %copy-start.2 = (bf16[512,3072]{1,0:T(8,128)(2,1)S(1)}, bf16[512,3072]{1,0:T(8,128)(2,1)}, u32[]{:S(2)}) copy-start(bf16[512,3072]{1,0:T(8,128)(2,1)} %get-tuple-element.15) | copy-start | bytes 9437188
  184.2 16.5 %copy-start.3 = (bf16[512,3072]{1,0:T(8,128)(2,1)S(1)}, bf16[512,3072]{1,0:T(8,128)(2,1)}, u32[]{:S(2)}) copy-start(bf16[512,3072]{1,0:T(8,128)(2,1)} %get-tuple-element.14) | copy-start | bytes 9437188
  200.7 13.3 %copy-start.1 = (bf16[64,3072]{1,0:T(8,128)(2,1)S(1)}, bf16[64,3072]{1,0:T(8,128)(2,1)}, u32[]{:S(2)}) copy-start(bf16[64,3072]{1,0:T(8,128)(2,1)} %get-tuple-element.20) | copy-start | bytes 1179652
  200.7 14.1 %copy-start = (bf16[64,3072]{1,0:T(8,128)(2,1)S(1)}, bf16[64,3072]{1,0:T(8,128)(2,1)}, u32[]{:S(2)}) copy-start(bf16[64,3072]{1,0:T(8,128)(2,1)} %get-tuple-element.21) | copy-start | bytes 1179652
